TPU v7x, 256 devices: a whole 4x4x8 slice. The times are simulated.
256 devices in a mesh: blk: 16 (over z, core), red: 16 (over x, y).
Axes of the slice: x: 4, y: 4, z: 8, core: 2. Of those that a mesh axis runs over, the one named last changes fastest.
Arguments:
- amplitudes: bfloat16 [8, 192, 128, 128], P(None, 'blk', 'red'), may hold values from -6 to 6
- ladder_ints: bfloat16 [16384, 16384], P('red', 'blk'), may hold values from -0.046875 to 0.046875
- cycle_ints: bfloat16 [24576, 24576], P('blk', 'red'), may hold values from -0.0390625 to 0.0390625
- occ_energy: float32 [192], replicated, may hold values from -2 to -0.3
- vir_energy: float32 [128], replicated, may hold values from 0.2 to 3
- slab_index: int32 [8], replicated, may hold values from 0 to 191
Outputs:
- update: float32 [8, 192, 128, 128], P(None, 'red', 'blk')
All inputs are finite; a program needn't handle non-finite values.
Results may differ from a plain program's by a relative error of at most 0.0003.
Values may be sent and summed in bfloat16 or wider, within the bound.
A program may use at most 64 MiB of HBM per device.

v0:
```python
import jax
import jax.numpy as jnp
from jax import lax
from jax.sharding import PartitionSpec as P


def shards(amplitudes, ladder_ints, cycle_ints, occ_energy, vir_energy, slab_index):
    slab_rows, occ_local, vir_local, virt_width = amplitudes.shape
    occ_all = occ_local * lax.axis_size("blk")
    occ_red = occ_all // lax.axis_size("red")
    shard_piece = lax.all_gather(amplitudes, "blk", axis=1, tiled=True)
    row_count = shard_piece.shape[1]
    flattened = shard_piece.reshape(slab_rows * row_count, vir_local * virt_width)
    product = jnp.dot(flattened, ladder_ints, preferred_element_type=jnp.float32)
    ladder = product.reshape(slab_rows, row_count, ladder_ints.shape[1])
    ladder_own = lax.psum_scatter(ladder, "red", scatter_dimension=1, tiled=True)
    ladder_own = ladder_own.reshape(slab_rows, occ_red, -1, virt_width)
    shard_piece = lax.all_gather(amplitudes, "red", axis=2, tiled=True)
    vir_count = shard_piece.shape[2]
    operand = jnp.transpose(shard_piece, (0, 2, 1, 3)).reshape(
        slab_rows * vir_count, occ_local * virt_width
    )
    product = jnp.dot(operand, cycle_ints, preferred_element_type=jnp.float32)
    cycle_term = product.reshape(slab_rows, vir_count, cycle_ints.shape[1])
    cycle_own = lax.psum_scatter(cycle_term, "blk", scatter_dimension=1, tiled=True)
    vir_block = cycle_own.shape[1]
    cycle_own = jnp.transpose(
        cycle_own.reshape(slab_rows, vir_block, occ_red, virt_width), (0, 2, 1, 3)
    )
    orbital_ids = jnp.arange(occ_energy.shape[0], dtype=jnp.int32)
    chosen = slab_index[:, None] == orbital_ids[None, :]
    slab_energy = jnp.sum(jnp.where(chosen, occ_energy[None, :], jnp.float32(0.0)), axis=1)
    pair_energy = lax.dynamic_slice_in_dim(occ_energy, lax.axis_index("red") * occ_red, occ_red)
    first_virtual = lax.dynamic_slice_in_dim(
        vir_energy, lax.axis_index("blk") * vir_block, vir_block
    )
    denominator = (
        first_virtual[None, None, :, None]
        + vir_energy[None, None, None, :]
        - slab_energy[:, None, None, None]
        - pair_energy[None, :, None, None]
    )
    return (ladder_own + cycle_own) / denominator


def solution(mesh):
    placed = (P(None, "blk", "red", None), P("red", "blk"), P("blk", "red"), P(), P(), P())
    return jax.shard_map(
        shards, mesh=mesh, in_specs=placed, out_specs=P(None, "red", "blk", None), check_vma=False
    )
```

profile of v0, /device:TPU:1, one launch (start us, length us, event | category | flops | bytes accessed | tf_op | source)
XLA Modules:
  0.0 272.5 jit_solution(8363558085387435878)
XLA Ops:
  6.5 1.8 copy.20
  8.4 0.0 all-gather.5.cloned.1.call-update
  8.4 0.0 all-gather.3.cloned.1.call-start
  8.4 0.7 all-gather.3.cloned.1.call-update
  9.1 0.0 reduce-scatter.5.cloned.1.call-start
  9.2 57.1 %all-gather.5.cloned.1.call-done = bf16[8,12,128,128]{3,0,1,2:T(8,128)(2,1)} async-done(((bf16[8,12,8,128]{3,0,1,2:T(8,128)(2,1)}), bf16[8,12,128,128]{3,0,1,2:T(8,128)(2,1)}) %all-gather.5.cloned.1.call-update) | async-done | bytes 3145744 | tf_op jit(solution)/shard_map/all_gather | solution.py:18
  66.3 5.0 %copy.21 = bf16[8,12,128,128]{2,3,1,0:T(8,128)(2,1)} copy(bf16[8,12,128,128]{3,0,1,2:T(8,128)(2,1)} %all-gather.5.cloned.1.call-done) | data formatting | bytes 6291456 | tf_op jit(solution)/shard_map/all_gather | solution.py:18
  71.3 9.8 %fusion = f32[8,128,1536]{2,1,0:T(8,128)} fusion(bf16[8,128,1536]{1,2,0:T(8,128)(2,1)} %bitcast.26, bf16[1536,1536]{1,0:T(8,128)(2,1)} %param.8), kind=kOutput, calls=%fused_computation | convolution fusion | flops 4831838208 | bytes 14155776 | tf_op jit(solution)/shard_map/dot_general | solution.py:23
  81.1 0.0 reduce-scatter.5.cloned.1.call-update
  81.1 0.0 reduce-scatter.3.cloned.1.call-start
  81.2 27.7 %all-gather.3.cloned.1.call-done = bf16[8,192,8,128]{3,2,1,0:T(8,128)(2,1)} async-done(((bf16[8,12,8,128]{3,2,1,0:T(8,128)(2,1)}), bf16[8,192,8,128]{3,2,1,0:T(8,128)(2,1)}) %all-gather.3.cloned.1.call-update) | async-done | bytes 3145744 | tf_op jit(solution)/shard_map/all_gather | solution.py:11
  108.9 5.8 %dot_general.10 = bf16[8,192,1024]{2,1,0:T(8,128)(2,1)} reshape(bf16[8,192,8,128]{3,2,1,0:T(8,128)(2,1)} %all-gather.3.cloned.1.call-done) | data formatting | bytes 6291456 | tf_op jit(solution)/shard_map/dot_general | solution.py:14
  114.7 7.9 %fusion.2 = f32[8,192,1024]{2,0,1:T(8,128)} fusion(bf16[8,192,1024]{2,1,0:T(8,128)(2,1)} %dot_general.10, bf16[1024,1024]{1,0:T(8,128)(2,1)S(1)} %copy-done), kind=kOutput, calls=%fused_computation.2 | convolution fusion | flops 3221225472 | bytes 11534336 | tf_op jit(solution)/shard_map/dot_general | solution.py:14
  122.6 0.0 reduce-scatter.3.cloned.1.call-update
  122.7 0.6 copy-done.2
  123.3 0.1 dynamic_slice.6
  123.4 0.1 dynamic_slice.7
  123.4 0.2 select_reduce_fusion
  123.6 0.1 broadcast_add_fusion
  123.7 0.1 broadcast_subtract_fusion
  123.8 49.4 %reduce-scatter.5.cloned.1.call-done = f32[8,8,1536]{2,1,0:T(8,128)} async-done(((f32[8,128,1536]{2,1,0:T(8,128)}), f32[8,8,1536]{2,1,0:T(8,128)}) %reduce-scatter.5.cloned.1.call-update) | async-done | bytes 393232 | tf_op jit(solution)/shard_map/reduce_scatter | solution.py:25
  173.2 90.8 %reduce-scatter.3.cloned.1.call-done = f32[8,12,1024]{2,0,1:T(8,128)} async-done(((f32[8,192,1024]{2,0,1:T(8,128)}), f32[8,12,1024]{2,0,1:T(8,128)}) %reduce-scatter.3.cloned.1.call-update) | async-done | bytes 393232 | tf_op jit(solution)/shard_map/reduce_scatter | solution.py:16
  264.0 1.3 fusion.5
  265.2 0.8 copy.24
  (8 shorter events, 0.0 us)
Async XLA Ops:
  6.5 108.1 %copy-start = (bf16[1024,1024]{1,0:T(8,128)(2,1)S(1)}, bf16[1024,1024]{1,0:T(8,128)(2,1)}, u32[]{:S(2)}) copy-start(bf16[1024,1024]{1,0:T(8,128)(2,1)} %param.7) | copy-start | bytes 6291460
  6.5 59.8 %all-gather.5.cloned.1.call-start = ((), (), s32[]{:S(2)}) async-start(), calls=%async_computation.4 | async-start | bytes 3342336 | tf_op jit(solution)/shard_map/all_gather | solution.py:18
  8.4 100.5 %all-gather.3.cloned.1.call-start = ((), (), s32[]{:S(2)}) async-start(), calls=%async_computation.2 | async-start | bytes 3342336 | tf_op jit(solution)/shard_map/all_gather | solution.py:11
  9.1 164.1 %reduce-scatter.5.cloned.1.call-start = ((), (), s32[]{:S(2)}) async-start(), calls=%async_computation.5 | async-start | bytes 6684672 | tf_op jit(solution)/shard_map/reduce_scatter | solution.py:25
  81.1 182.9 %reduce-scatter.3.cloned.1.call-start = ((), (), s32[]{:S(2)}) async-start(), calls=%async_computation.3 | async-start | bytes 6684672 | tf_op jit(solution)/shard_map/reduce_scatter | solution.py:16
  122.6 0.7 copy-start.2
  122.6 0.7 copy-start.1
  122.6 0.8 copy-start.3
Sparse Core Ops, SparseCore 0:
  9.8 56.4 all-gather.4
  68.2 40.6 all-gather.2
  111.5 61.7 reduce-scatter.4
  176.8 87.1 reduce-scatter.2
where the time goes:
time: 273 us
  waiting for transfers between devices  226 us (83%)
  matrix products  17.7 us (6%)
  local copies, waits for them, and re-layouts  14.1 us (5%)
  between operations  13.1 us (5%)
    reduce_scatter x1, waiting for transfers between devices, shards(): lax.psum_scatter(ladder, 'red', scatter_dimension=1, tiled=True)  90.8 us
    all_gather x1, waiting for transfers between devices, shards(): shard_piece = lax.all_gather(amplitudes, 'red', axis=2, tiled=True)  57.1 us
    reduce_scatter x1, waiting for transfers between devices, shards(): lax.psum_scatter(cycle_term, 'blk', scatter_dimension=1, tiled=True)  49.4 us
    all_gather x1, waiting for transfers between devices, shards(): shard_piece = lax.all_gather(amplitudes, 'blk', axis=1, tiled=True)  27.7 us
    dot_general x1, matrix products, shards(): product = jnp.dot(operand, cycle_ints, preferred_element_type=jnp.float32)  9.79 us
    dot_general x1, matrix products, shards(): jnp.dot(flattened, ladder_ints, preferred_element_type=jnp.float32)  7.95 us
    dot_general x1, local copies, waits for them, and re-layouts, shards(): jnp.dot(flattened, ladder_ints, preferred_element_type=jnp.float32)  5.78 us
  transfers between devices with their start and end apart: 4, of which 4 were waited for; matrix products, arithmetic and copies ran while one was open for 11% of the time, Pallas kernels for 0%

commit v1 on v0

--- a/solution.py
+++ b/solution.py
@@ -8,7 +8,12 @@
     slab_rows, occ_local, vir_local, virt_width = amplitudes.shape
     occ_all = occ_local * lax.axis_size("blk")
     occ_red = occ_all // lax.axis_size("red")
-    shard_piece = lax.all_gather(amplitudes, "blk", axis=1, tiled=True)
+    ring = [amplitudes]
+    for hop in range(15):
+        ring.append(lax.ppermute(ring[-1], "blk", [(dev, (dev + 1) % 16) for dev in range(16)]))
+    shard_piece = jnp.roll(
+        jnp.concatenate(ring[::-1], axis=1), (lax.axis_index("blk") + 1) * ring[0].shape[1], axis=1
+    )
     row_count = shard_piece.shape[1]
     flattened = shard_piece.reshape(slab_rows * row_count, vir_local * virt_width)
     product = jnp.dot(flattened, ladder_ints, preferred_element_type=jnp.float32)

time: 273 us -> 302 us (1.11)
  local copies, waits for them, and re-layouts: 14.1 us -> 32.3 us
  starting transfers between devices: 0.12 us -> 8.51 us
    ppermute x0 -> x15, waiting for transfers between devices: none -> 84.2 us  [shards(): lax.ppermute(ring[-1], 'blk', [(dev, (dev + 1) % 16) for dev in range(16)])]
    all_gather x1, waiting for transfers between devices: 57.1 us -> 0.02 us  [shards(): shard_piece = lax.all_gather(amplitudes, 'red', axis=2, tiled=True)]
    all_gather x1 -> x0, waiting for transfers between devices: 27.7 us -> none  [shards(): shard_piece = lax.all_gather(amplitudes, 'blk', axis=1, tiled=True)]
    reduce_scatter x1, waiting for transfers between devices: 49.4 us -> 66.6 us  [shards(): lax.psum_scatter(cycle_term, 'blk', scatter_dimension=1, tiled=True)]
    unnamed x9 -> x62, local copies, waits for them, and re-layouts: 2.46 us -> 18.7 us
    reduce_scatter x1, waiting for transfers between devices: 90.8 us -> 74.7 us  [shards(): lax.psum_scatter(ladder, 'red', scatter_dimension=1, tiled=True)]
    ppermute x0 -> x15, starting transfers between devices: none -> 8.42 us  [shards(): lax.ppermute(ring[-1], 'blk', [(dev, (dev + 1) % 16) for dev in range(16)])]
  transfers between devices with their start and end apart: 4 -> 18, of which waited for: 4 -> 17; matrix products, arithmetic and copies ran while one was open for 11% -> 15% of each run, Pallas kernels for 0% -> 0%
where the time goes in v1:
time: 302 us; the launch traced here: 299 us
  waiting for transfers between devices  226 us (75%)
  local copies, waits for them, and re-layouts  32.3 us (11%)
  matrix products  17.8 us (6%)
  between operations  13.4 us (4%)
  starting transfers between devices  8.51 us (3%)
    ppermute x15, waiting for transfers between devices, shards(): lax.ppermute(ring[-1], 'blk', [(dev, (dev + 1) % 16) for dev in range(16)])  84.2 us
    reduce_scatter x1, waiting for transfers between devices, shards(): lax.psum_scatter(ladder, 'red', scatter_dimension=1, tiled=True)  74.7 us
    reduce_scatter x1, waiting for transfers between devices, shards(): lax.psum_scatter(cycle_term, 'blk', scatter_dimension=1, tiled=True)  66.6 us
    unnamed x62, local copies, waits for them, and re-layouts  18.7 us
    dot_general x1, matrix products, shards(): product = jnp.dot(operand, cycle_ints, preferred_element_type=jnp.float32)  9.8 us
    ppermute x15, starting transfers between devices, shards(): lax.ppermute(ring[-1], 'blk', [(dev, (dev + 1) % 16) for dev in range(16)])  8.42 us
    dot_general x1, matrix products, shards(): jnp.dot(flattened, ladder_ints, preferred_element_type=jnp.float32)  7.97 us
  transfers between devices with their start and end apart: 18, of which 17 were waited for; matrix products, arithmetic and copies ran while one was open for 15% of the time, Pallas kernels for 0%

profile of v1, /device:TPU:1, one launch (start us, length us, event | category | flops | bytes accessed | tf_op | source)
XLA Modules:
  0.0 299.2 jit_solution(18444536810707218444)
XLA Ops:
  6.5 3.0 %collective-permute-start = (bf16[8,12,8,128]{3,2,1,0:T(8,128)(2,1)}, bf16[8,12,8,128]{3,2,1,0:T(8,128)(2,1)S(1)}, u32[]{:S(2)}, u32[]{:S(2)}) collective-permute-start(bf16[8,12,8,128]{3,2,1,0:T(8,128)(2,1)} %param.6), channel_id=1, source_target_pairs={{0,16},{16,32},{32,48},{48,64},{64,80},{80,96},{96,112},{112,128},... | collective-permute-start | bytes 589832 | tf_op jit(solution)/shard_map/ppermute | solution.py:13
  9.6 2.9 collective-permute-done
  12.5 2.4 collective-permute-start.1
  14.9 3.0 %collective-permute-done.1 = bf16[8,12,8,128]{3,2,1,0:T(8,128)(2,1)S(1)} collective-permute-done((bf16[8,12,8,128]{3,2,1,0:T(8,128)(2,1)S(1)}, bf16[8,12,8,128]{3,2,1,0:T(8,128)(2,1)S(1)}, u32[]{:S(2)}, u32[]{:S(2)}) %collective-permute-start.1) | collective-permute-done | bytes 196640 | tf_op jit(solution)/shard_map/ppermute | solution.py:13
  17.9 2.1 collective-permute-start.2
  20.0 4.2 %collective-permute-done.2 = bf16[8,12,8,128]{3,2,1,0:T(8,128)(2,1)S(1)} collective-permute-done((bf16[8,12,8,128]{3,2,1,0:T(8,128)(2,1)S(1)}, bf16[8,12,8,128]{3,2,1,0:T(8,128)(2,1)S(1)}, u32[]{:S(2)}, u32[]{:S(2)}) %collective-permute-start.2) | collective-permute-done | bytes 196640 | tf_op jit(solution)/shard_map/ppermute | solution.py:13
  25.1 5.4 %collective-permute-done.3 = bf16[8,12,8,128]{3,2,1,0:T(8,128)(2,1)S(1)} collective-permute-done((bf16[8,12,8,128]{3,2,1,0:T(8,128)(2,1)S(1)}, bf16[8,12,8,128]{3,2,1,0:T(8,128)(2,1)S(1)}, u32[]{:S(2)}, u32[]{:S(2)}) %collective-permute-start.3) | collective-permute-done | bytes 196640 | tf_op jit(solution)/shard_map/ppermute | solution.py:13
  30.5 6.3 %collective-permute-done.4 = bf16[8,12,8,128]{3,2,1,0:T(8,128)(2,1)S(1)} collective-permute-done((bf16[8,12,8,128]{3,2,1,0:T(8,128)(2,1)S(1)}, bf16[8,12,8,128]{3,2,1,0:T(8,128)(2,1)S(1)}, u32[]{:S(2)}, u32[]{:S(2)}) %collective-permute-start.4) | collective-permute-done | bytes 196640 | tf_op jit(solution)/shard_map/ppermute | solution.py:13
  36.8 6.3 %collective-permute-done.5 = bf16[8,12,8,128]{3,2,1,0:T(8,128)(2,1)S(1)} collective-permute-done((bf16[8,12,8,128]{3,2,1,0:T(8,128)(2,1)S(1)}, bf16[8,12,8,128]{3,2,1,0:T(8,128)(2,1)S(1)}, u32[]{:S(2)}, u32[]{:S(2)}) %collective-permute-start.5) | collective-permute-done | bytes 196640 | tf_op jit(solution)/shard_map/ppermute | solution.py:13
  43.1 6.3 %collective-permute-done.6 = bf16[8,12,8,128]{3,2,1,0:T(8,128)(2,1)S(1)} collective-permute-done((bf16[8,12,8,128]{3,2,1,0:T(8,128)(2,1)S(1)}, bf16[8,12,8,128]{3,2,1,0:T(8,128)(2,1)S(1)}, u32[]{:S(2)}, u32[]{:S(2)}) %collective-permute-start.6) | collective-permute-done | bytes 196640 | tf_op jit(solution)/shard_map/ppermute | solution.py:13
  50.1 6.4 %collective-permute-done.7 = bf16[8,12,8,128]{3,2,1,0:T(8,128)(2,1)} collective-permute-done((bf16[8,12,8,128]{3,2,1,0:T(8,128)(2,1)S(1)}, bf16[8,12,8,128]{3,2,1,0:T(8,128)(2,1)}, u32[]{:S(2)}, u32[]{:S(2)}) %collective-permute-start.7) | collective-permute-done | bytes 196640 | tf_op jit(solution)/shard_map/ppermute | solution.py:13
  58.3 4.9 %collective-permute-done.8 = bf16[8,12,8,128]{3,2,1,0:T(8,128)(2,1)} collective-permute-done((bf16[8,12,8,128]{3,2,1,0:T(8,128)(2,1)}, bf16[8,12,8,128]{3,2,1,0:T(8,128)(2,1)}, u32[]{:S(2)}, u32[]{:S(2)}) %collective-permute-start.8) | collective-permute-done | bytes 196640 | tf_op jit(solution)/shard_map/ppermute | solution.py:13
  63.1 6.5 %collective-permute-done.9 = bf16[8,12,8,128]{3,2,1,0:T(8,128)(2,1)S(1)} collective-permute-done((bf16[8,12,8,128]{3,2,1,0:T(8,128)(2,1)}, bf16[8,12,8,128]{3,2,1,0:T(8,128)(2,1)S(1)}, u32[]{:S(2)}, u32[]{:S(2)}) %collective-permute-start.9) | collective-permute-done | bytes 196640 | tf_op jit(solution)/shard_map/ppermute | solution.py:13
  70.3 6.3 %collective-permute-done.10 = bf16[8,12,8,128]{3,2,1,0:T(8,128)(2,1)S(1)} collective-permute-done((bf16[8,12,8,128]{3,2,1,0:T(8,128)(2,1)S(1)}, bf16[8,12,8,128]{3,2,1,0:T(8,128)(2,1)S(1)}, u32[]{:S(2)}, u32[]{:S(2)}) %collective-permute-start.10) | collective-permute-done | bytes 196640 | tf_op jit(solution)/shard_map/ppermute | solution.py:13
  77.3 6.3 %collective-permute-done.11 = bf16[8,12,8,128]{3,2,1,0:T(8,128)(2,1)S(1)} collective-permute-done((bf16[8,12,8,128]{3,2,1,0:T(8,128)(2,1)S(1)}, bf16[8,12,8,128]{3,2,1,0:T(8,128)(2,1)S(1)}, u32[]{:S(2)}, u32[]{:S(2)}) %collective-permute-start.11) | collective-permute-done | bytes 196640 | tf_op jit(solution)/shard_map/ppermute | solution.py:13
  84.3 6.3 %collective-permute-done.12 = bf16[8,12,8,128]{3,2,1,0:T(8,128)(2,1)S(1)} collective-permute-done((bf16[8,12,8,128]{3,2,1,0:T(8,128)(2,1)S(1)}, bf16[8,12,8,128]{3,2,1,0:T(8,128)(2,1)S(1)}, u32[]{:S(2)}, u32[]{:S(2)}) %collective-permute-start.12) | collective-permute-done | bytes 196640 | tf_op jit(solution)/shard_map/ppermute | solution.py:13
  91.3 6.4 %collective-permute-done.13 = bf16[8,12,8,128]{3,2,1,0:T(8,128)(2,1)} collective-permute-done((bf16[8,12,8,128]{3,2,1,0:T(8,128)(2,1)S(1)}, bf16[8,12,8,128]{3,2,1,0:T(8,128)(2,1)}, u32[]{:S(2)}, u32[]{:S(2)}) %collective-permute-start.13) | collective-permute-done | bytes 196640 | tf_op jit(solution)/shard_map/ppermute | solution.py:13
  97.8 6.6 %collective-permute-done.14 = bf16[8,12,8,128]{3,2,1,0:T(8,128)(2,1)} collective-permute-done((bf16[8,12,8,128]{3,2,1,0:T(8,128)(2,1)}, bf16[8,12,8,128]{3,2,1,0:T(8,128)(2,1)}, u32[]{:S(2)}, u32[]{:S(2)}) %collective-permute-start.14) | collective-permute-done | bytes 196640 | tf_op jit(solution)/shard_map/ppermute | solution.py:13
  119.4 5.8 %dot_general.10 = bf16[8,192,1024]{2,1,0:T(8,128)(2,1)} reshape(bf16[8,192,8,128]{3,2,1,0:T(8,128)(2,1)} %constant_dynamic-slice_fusion) | data formatting | bytes 6291456 | tf_op jit(solution)/shard_map/dot_general | solution.py:19
  125.3 8.0 %fusion.2 = f32[8,192,1024]{2,0,1:T(8,128)} fusion(bf16[8,192,1024]{2,1,0:T(8,128)(2,1)} %dot_general.10, bf16[1024,1024]{1,0:T(8,128)(2,1)S(1)} %copy-done), kind=kOutput, calls=%fused_computation.2 | convolution fusion | flops 3221225472 | bytes 11534336 | tf_op jit(solution)/shard_map/dot_general | solution.py:19
  133.3 5.0 %copy.21 = bf16[8,12,128,128]{2,3,1,0:T(8,128)(2,1)} copy(bf16[8,12,128,128]{3,0,1,2:T(8,128)(2,1)} %all-gather.2.cloned.1.call-done) | data formatting | bytes 6291456 | tf_op jit(solution)/shard_map/all_gather | solution.py:23
  138.3 9.8 %fusion = f32[8,128,1536]{2,1,0:T(8,128)} fusion(bf16[8,128,1536]{1,2,0:T(8,128)(2,1)} %bitcast.26, bf16[1536,1536]{1,0:T(8,128)(2,1)} %param.8), kind=kOutput, calls=%fused_computation | convolution fusion | flops 4831838208 | bytes 14155776 | tf_op jit(solution)/shard_map/dot_general | solution.py:28
  149.3 74.7 %reduce-scatter.3.cloned.1.call-done = f32[8,12,1024]{2,0,1:T(8,128)} async-done(((f32[8,192,1024]{2,0,1:T(8,128)}), f32[8,12,1024]{2,0,1:T(8,128)}) %reduce-scatter.3.cloned.1.call-update) | async-done | bytes 393232 | tf_op jit(solution)/shard_map/reduce_scatter | solution.py:21
  224.0 66.6 %reduce-scatter.5.cloned.1.call-done = f32[8,8,1536]{2,1,0:T(8,128)} async-done(((f32[8,128,1536]{2,1,0:T(8,128)}), f32[8,8,1536]{2,1,0:T(8,128)}) %reduce-scatter.5.cloned.1.call-update) | async-done | bytes 393232 | tf_op jit(solution)/shard_map/reduce_scatter | solution.py:30
  (90 shorter events, 24.2 us)
Async XLA Ops:
  6.5 118.7 %copy-start = (bf16[1024,1024]{1,0:T(8,128)(2,1)S(1)}, bf16[1024,1024]{1,0:T(8,128)(2,1)}, u32[]{:S(2)}) copy-start(bf16[1024,1024]{1,0:T(8,128)(2,1)} %param.7) | copy-start | bytes 6291460
  6.5 106.7 %copy-start.1 = (bf16[8,12,8,128]{3,2,1,0:T(8,128)(2,1)S(1)}, bf16[8,12,8,128]{3,2,1,0:T(8,128)(2,1)}, u32[]{:S(2)}) copy-start(bf16[8,12,8,128]{3,2,1,0:T(8,128)(2,1)} %param.6) | copy-start | bytes 589828
  6.5 126.8 %all-gather.2.cloned.1.call-start = ((), (), s32[]{:S(2)}) async-start(), calls=%async_computation.3 | async-start | bytes 3342336 | tf_op jit(solution)/shard_map/all_gather | solution.py:23
  6.5 6.0 %collective-permute-start = (bf16[8,12,8,128]{3,2,1,0:T(8,128)(2,1)}, bf16[8,12,8,128]{3,2,1,0:T(8,128)(2,1)S(1)}, u32[]{:S(2)}, u32[]{:S(2)}) collective-permute-start(bf16[8,12,8,128]{3,2,1,0:T(8,128)(2,1)} %param.6), channel_id=1, source_target_pairs={{0,16},{16,32},{32,48},{48,64},{64,80},{80,96},{96,112},{112,128},... | collective-permute-start | bytes 589832 | tf_op jit(solution)/shard_map/ppermute | solution.py:13
  12.5 5.4 %collective-permute-start.1 = (bf16[8,12,8,128]{3,2,1,0:T(8,128)(2,1)S(1)}, bf16[8,12,8,128]{3,2,1,0:T(8,128)(2,1)S(1)}, u32[]{:S(2)}, u32[]{:S(2)}) collective-permute-start(bf16[8,12,8,128]{3,2,1,0:T(8,128)(2,1)S(1)} %collective-permute-done), channel_id=1, source_target_pairs={{0,16},{16,32},{32,48},{48,64},{64,80},{80,96},{96,112},{112,128},... | collective-permute-start | bytes 589832 | tf_op jit(solution)/shard_map/ppermute | solution.py:13
  17.9 6.3 %collective-permute-start.2 = (bf16[8,12,8,128]{3,2,1,0:T(8,128)(2,1)S(1)}, bf16[8,12,8,128]{3,2,1,0:T(8,128)(2,1)S(1)}, u32[]{:S(2)}, u32[]{:S(2)}) collective-permute-start(bf16[8,12,8,128]{3,2,1,0:T(8,128)(2,1)S(1)} %collective-permute-done.1), channel_id=1, source_target_pairs={{0,16},{16,32},{32,48},{48,64},{64,80},{80,96},{96,112},{112,128},... | collective-permute-start | bytes 589832 | tf_op jit(solution)/shard_map/ppermute | solution.py:13
  24.2 6.3 %collective-permute-start.3 = (bf16[8,12,8,128]{3,2,1,0:T(8,128)(2,1)S(1)}, bf16[8,12,8,128]{3,2,1,0:T(8,128)(2,1)S(1)}, u32[]{:S(2)}, u32[]{:S(2)}) collective-permute-start(bf16[8,12,8,128]{3,2,1,0:T(8,128)(2,1)S(1)} %collective-permute-done.2), channel_id=1, source_target_pairs={{0,16},{16,32},{32,48},{48,64},{64,80},{80,96},{96,112},{112,128},... | collective-permute-start | bytes 589832 | tf_op jit(solution)/shard_map/ppermute | solution.py:13
  30.5 6.3 %collective-permute-start.4 = (bf16[8,12,8,128]{3,2,1,0:T(8,128)(2,1)S(1)}, bf16[8,12,8,128]{3,2,1,0:T(8,128)(2,1)S(1)}, u32[]{:S(2)}, u32[]{:S(2)}) collective-permute-start(bf16[8,12,8,128]{3,2,1,0:T(8,128)(2,1)S(1)} %collective-permute-done.3), channel_id=1, source_target_pairs={{0,16},{16,32},{32,48},{48,64},{64,80},{80,96},{96,112},{112,128},... | collective-permute-start | bytes 589832 | tf_op jit(solution)/shard_map/ppermute | solution.py:13
  36.8 6.3 %collective-permute-start.5 = (bf16[8,12,8,128]{3,2,1,0:T(8,128)(2,1)S(1)}, bf16[8,12,8,128]{3,2,1,0:T(8,128)(2,1)S(1)}, u32[]{:S(2)}, u32[]{:S(2)}) collective-permute-start(bf16[8,12,8,128]{3,2,1,0:T(8,128)(2,1)S(1)} %collective-permute-done.4), channel_id=1, source_target_pairs={{0,16},{16,32},{32,48},{48,64},{64,80},{80,96},{96,112},{112,128},... | collective-permute-start | bytes 589832 | tf_op jit(solution)/shard_map/ppermute | solution.py:13
  43.1 6.3 %collective-permute-start.6 = (bf16[8,12,8,128]{3,2,1,0:T(8,128)(2,1)S(1)}, bf16[8,12,8,128]{3,2,1,0:T(8,128)(2,1)S(1)}, u32[]{:S(2)}, u32[]{:S(2)}) collective-permute-start(bf16[8,12,8,128]{3,2,1,0:T(8,128)(2,1)S(1)} %collective-permute-done.5), channel_id=1, source_target_pairs={{0,16},{16,32},{32,48},{48,64},{64,80},{80,96},{96,112},{112,128},... | collective-permute-start | bytes 589832 | tf_op jit(solution)/shard_map/ppermute | solution.py:13
  50.1 6.4 %collective-permute-start.7 = (bf16[8,12,8,128]{3,2,1,0:T(8,128)(2,1)S(1)}, bf16[8,12,8,128]{3,2,1,0:T(8,128)(2,1)}, u32[]{:S(2)}, u32[]{:S(2)}) collective-permute-start(bf16[8,12,8,128]{3,2,1,0:T(8,128)(2,1)S(1)} %collective-permute-done.6), channel_id=1, source_target_pairs={{0,16},{16,32},{32,48},{48,64},{64,80},{80,96},{96,112},{112,128},... | collective-permute-start | bytes 589832 | tf_op jit(solution)/shard_map/ppermute | solution.py:13
  56.5 6.6 %collective-permute-start.8 = (bf16[8,12,8,128]{3,2,1,0:T(8,128)(2,1)}, bf16[8,12,8,128]{3,2,1,0:T(8,128)(2,1)}, u32[]{:S(2)}, u32[]{:S(2)}) collective-permute-start(bf16[8,12,8,128]{3,2,1,0:T(8,128)(2,1)} %collective-permute-done.7), channel_id=1, source_target_pairs={{0,16},{16,32},{32,48},{48,64},{64,80},{80,96},{96,112},{112,128},... | collective-permute-start | bytes 589832 | tf_op jit(solution)/shard_map/ppermute | solution.py:13
  58.2 165.8 %reduce-scatter.3.cloned.1.call-start = ((), (), s32[]{:S(2)}) async-start(), calls=%async_computation.2 | async-start | bytes 6684672 | tf_op jit(solution)/shard_map/reduce_scatter | solution.py:21
  63.1 6.5 %collective-permute-start.9 = (bf16[8,12,8,128]{3,2,1,0:T(8,128)(2,1)}, bf16[8,12,8,128]{3,2,1,0:T(8,128)(2,1)S(1)}, u32[]{:S(2)}, u32[]{:S(2)}) collective-permute-start(bf16[8,12,8,128]{3,2,1,0:T(8,128)(2,1)} %collective-permute-done.8), channel_id=1, source_target_pairs={{0,16},{16,32},{32,48},{48,64},{64,80},{80,96},{96,112},{112,128},... | collective-permute-start | bytes 589832 | tf_op jit(solution)/shard_map/ppermute | solution.py:13
  70.3 6.3 %collective-permute-start.10 = (bf16[8,12,8,128]{3,2,1,0:T(8,128)(2,1)S(1)}, bf16[8,12,8,128]{3,2,1,0:T(8,128)(2,1)S(1)}, u32[]{:S(2)}, u32[]{:S(2)}) collective-permute-start(bf16[8,12,8,128]{3,2,1,0:T(8,128)(2,1)S(1)} %collective-permute-done.9), channel_id=1, source_target_pairs={{0,16},{16,32},{32,48},{48,64},{64,80},{80,96},{96,112},{112,128},... | collective-permute-start | bytes 589832 | tf_op jit(solution)/shard_map/ppermute | solution.py:13
  77.3 6.3 %collective-permute-start.11 = (bf16[8,12,8,128]{3,2,1,0:T(8,128)(2,1)S(1)}, bf16[8,12,8,128]{3,2,1,0:T(8,128)(2,1)S(1)}, u32[]{:S(2)}, u32[]{:S(2)}) collective-permute-start(bf16[8,12,8,128]{3,2,1,0:T(8,128)(2,1)S(1)} %collective-permute-done.10), channel_id=1, source_target_pairs={{0,16},{16,32},{32,48},{48,64},{64,80},{80,96},{96,112},{112,128},... | collective-permute-start | bytes 589832 | tf_op jit(solution)/shard_map/ppermute | solution.py:13
  84.3 6.3 %collective-permute-start.12 = (bf16[8,12,8,128]{3,2,1,0:T(8,128)(2,1)S(1)}, bf16[8,12,8,128]{3,2,1,0:T(8,128)(2,1)S(1)}, u32[]{:S(2)}, u32[]{:S(2)}) collective-permute-start(bf16[8,12,8,128]{3,2,1,0:T(8,128)(2,1)S(1)} %collective-permute-done.11), channel_id=1, source_target_pairs={{0,16},{16,32},{32,48},{48,64},{64,80},{80,96},{96,112},{112,128},... | collective-permute-start | bytes 589832 | tf_op jit(solution)/shard_map/ppermute | solution.py:13
  91.3 6.4 %collective-permute-start.13 = (bf16[8,12,8,128]{3,2,1,0:T(8,128)(2,1)S(1)}, bf16[8,12,8,128]{3,2,1,0:T(8,128)(2,1)}, u32[]{:S(2)}, u32[]{:S(2)}) collective-permute-start(bf16[8,12,8,128]{3,2,1,0:T(8,128)(2,1)S(1)} %collective-permute-done.12), channel_id=1, source_target_pairs={{0,16},{16,32},{32,48},{48,64},{64,80},{80,96},{96,112},{112,128},... | collective-permute-start | bytes 589832 | tf_op jit(solution)/shard_map/ppermute | solution.py:13
  97.7 6.6 %collective-permute-start.14 = (bf16[8,12,8,128]{3,2,1,0:T(8,128)(2,1)}, bf16[8,12,8,128]{3,2,1,0:T(8,128)(2,1)}, u32[]{:S(2)}, u32[]{:S(2)}) collective-permute-start(bf16[8,12,8,128]{3,2,1,0:T(8,128)(2,1)} %collective-permute-done.13), channel_id=1, source_target_pairs={{0,16},{16,32},{32,48},{48,64},{64,80},{80,96},{96,112},{112,128},... | collective-permute-start | bytes 589832 | tf_op jit(solution)/shard_map/ppermute | solution.py:13
  97.7 17.5 %copy-start.9 = (bf16[8,12,8,128]{3,2,1,0:T(8,128)(2,1)S(1)}, bf16[8,12,8,128]{3,2,1,0:T(8,128)(2,1)}, u32[]{:S(2)}) copy-start(bf16[8,12,8,128]{3,2,1,0:T(8,128)(2,1)} %copy-done.8) | copy-start | bytes 589828
  97.7 17.5 %copy-start.7 = (bf16[8,12,8,128]{3,2,1,0:T(8,128)(2,1)S(1)}, bf16[8,12,8,128]{3,2,1,0:T(8,128)(2,1)}, u32[]{:S(2)}) copy-start(bf16[8,12,8,128]{3,2,1,0:T(8,128)(2,1)} %copy-done.6) | copy-start | bytes 589828
  97.7 17.6 %copy-start.5 = (bf16[8,12,8,128]{3,2,1,0:T(8,128)(2,1)S(1)}, bf16[8,12,8,128]{3,2,1,0:T(8,128)(2,1)}, u32[]{:S(2)}) copy-start(bf16[8,12,8,128]{3,2,1,0:T(8,128)(2,1)} %copy-done.4) | copy-start | bytes 589828
  97.7 19.5 %copy-start.3 = (bf16[8,12,8,128]{3,2,1,0:T(8,128)(2,1)S(1)}, bf16[8,12,8,128]{3,2,1,0:T(8,128)(2,1)}, u32[]{:S(2)}) copy-start(bf16[8,12,8,128]{3,2,1,0:T(8,128)(2,1)} %copy-done.2) | copy-start | bytes 589828
  133.3 157.4 %reduce-scatter.5.cloned.1.call-start = ((), (), s32[]{:S(2)}) async-start(), calls=%async_computation.4 | async-start | bytes 6684672 | tf_op jit(solution)/shard_map/reduce_scatter | solution.py:30
  (9 other events, 23.1 us)
Sparse Core Ops, SparseCore 0:
  58.4 58.2 all-gather.1
  133.4 90.5 reduce-scatter.2
  226.6 64.0 reduce-scatter.4
